TPU v7x, 32 devices: a whole 2x2x4 slice. The times are simulated.
32 devices in a mesh: bag: 4 (over y, x), seq: 8 (over z, core).
Axes of the slice: x: 2, y: 2, z: 4, core: 2. Of those that a mesh axis runs over, the one named last changes fastest.
Arguments:
- text_rows: bfloat16 [2048, 3072], P(('bag', 'seq')), may hold values from -6 to 6
- image_rows: bfloat16 [1024, 3072], P(('bag', 'seq')), may hold values from -6 to 6
- modulation: float32 [32, 2, 2, 3072], P('bag'), may hold values from -3 to 3
- head_weight: bfloat16 [2, 3072, 6144], P(None, None, 'seq'), may hold values from -0.109375 to 0.109375
- norm_gain: float32 [2, 2, 128], replicated, may hold values from 0.5 to 20
- store_down: bfloat16 [128, 2, 64, 3072], P('bag', None, 'seq'), may hold values from -0.109375 to 0.109375
- store_up: bfloat16 [128, 2, 64, 6144], P('bag', None, None, 'seq'), may hold values from -0.375 to 0.375
- store_row: int32 [128], replicated, may hold values from 0 to 127, as said below
- user_adapter: int32 [4, 4], replicated, may hold values from 0 to 127, as said below
- image_lengths: int32 [4, 4], P('bag'), may hold values from 1 to 64, 128 in all within a row
Outputs:
- text_out: bfloat16 [2048, 2048], P(('bag', 'seq'))
- image_out: bfloat16 [1024, 2048], P(('bag', 'seq'))
Inputs may be any that keep to these rules, and one draw needn't show every extreme that they name: A permutation: adapter a is kept at row store_row[a] of store_down and store_up, whose owner is store_row[a] // 32. `user_adapter`: the 4 users of one bag have adapters kept by 4 different owners, so every owner keeps exactly one adapter of each bag.
All inputs are finite; a program needn't handle non-finite values.
Results may differ from a plain program's by a relative error of at most 0.04.
The roundings to bfloat16 on the way count: a program that leaves them out, or rounds other values in their place, can miss the bound.
Values may be sent and summed in bfloat16 or wider, within the bound.
No kernel may reach another device: no remote copies, remote signals or barrier semaphores. Data moves between devices by JAX's collectives and lax.ppermute only.
A program may use at most 128 MiB of HBM per device.

v0:
```python
import math
import jax
import jax.numpy as jnp
from jax import lax
from jax.sharding import PartitionSpec as P

HEAD_DIM = 128
TEXT = 64


def modulate(raw_rows, shifts, scales):
    values = raw_rows.astype(jnp.float32)
    centre = values - jnp.mean(values, axis=-1, keepdims=True)
    spread = jnp.mean(centre * centre, axis=-1, keepdims=True)
    normed = centre * lax.rsqrt(spread + 1e-06)
    return ((1.0 + scales) * normed + shifts).astype(jnp.bfloat16)


def head_normed(values, gain_row):
    spread = jnp.mean(values * values, axis=-1, keepdims=True)
    return (values * lax.rsqrt(spread + 1e-06) * gain_row).astype(jnp.bfloat16)


def attend(queries, keys_all, values_all, seg_ids):
    row_total = queries.shape[0]
    block_rows = math.gcd(row_total, 1024)
    query_blocks = queries.reshape(row_total // block_rows, block_rows, queries.shape[1])
    seg_blocks = seg_ids.reshape(row_total // block_rows, block_rows)
    factor = 1.0 / math.sqrt(queries.shape[1])

    def one_block(block_pair):
        query_rows, query_segs = block_pair
        scores = jnp.dot(query_rows, keys_all.T, preferred_element_type=jnp.float32) * factor
        scores = jnp.where(query_segs[:, None] == seg_ids[None, :], scores, -1e30)
        top_score = jnp.max(scores, axis=1, keepdims=True)
        weights = jnp.exp(scores - top_score)
        prob_rows = (weights / jnp.sum(weights, axis=1, keepdims=True)).astype(jnp.bfloat16)
        return jnp.dot(prob_rows, values_all, preferred_element_type=jnp.float32).astype(
            jnp.bfloat16
        )

    return lax.map(one_block, (query_blocks, seg_blocks)).reshape(row_total, values_all.shape[1])


def user_table(user_ids, user_count):
    return user_ids[:, None] == jnp.arange(user_count, dtype=jnp.int32)[None, :]


def pick_rows(seg_pick, table_rows):
    return jnp.dot(seg_pick, table_rows, precision=lax.Precision.HIGHEST)


def part_ranks(hidden_all, down_part, user_ids, user_count):
    all_users = jnp.einsum("nd,urd->urn", hidden_all, down_part, preferred_element_type=jnp.float32)
    user_pick = user_table(user_ids, user_count).astype(jnp.float32).T
    return jnp.sum(all_users * user_pick[:, None, :], axis=0).astype(jnp.bfloat16)


def adapted(hidden_all, weight, ranks, up_users, user_ids, gain_pair):
    row_count = hidden_all.shape[0]
    user_count = up_users.shape[0]
    plain_part = jnp.dot(hidden_all, weight, preferred_element_type=jnp.float32)
    user_pick = user_table(user_ids, user_count).astype(jnp.bfloat16)
    spread_ranks = (user_pick[:, :, None] * ranks[:, None, :]).reshape(row_count, -1)
    adjust = jnp.dot(
        spread_ranks, up_users.reshape(-1, weight.shape[1]), preferred_element_type=jnp.float32
    )
    heads_here = weight.shape[1] // (3 * HEAD_DIM)
    mixed_cols = (plain_part + adjust).reshape(row_count, heads_here, 3, HEAD_DIM)
    query = head_normed(mixed_cols[:, :, 0], gain_pair[0])
    key_rows = head_normed(mixed_cols[:, :, 1], gain_pair[1])
    value_rows = mixed_cols[:, :, 2].astype(jnp.bfloat16)
    return (query, key_rows, value_rows)


def body(
    text_rows,
    image_rows,
    modulation,
    head_weight,
    norm_gain,
    store_down,
    store_up,
    store_row,
    user_adapter,
    image_lengths,
):
    seq_count = lax.axis_size("seq")
    bag_index = lax.axis_index("bag")
    seq_index = lax.axis_index("seq")
    text_dev = text_rows.shape[0]
    image_dev = image_rows.shape[0]
    text_bag = text_dev * seq_count
    image_bag = image_dev * seq_count
    user_count = image_lengths.shape[1]
    seg_count = modulation.shape[0]
    store_size = store_down.shape[0]
    seg_ends = jnp.cumsum(jnp.repeat(image_lengths[0], 2))
    text_segs = jnp.arange(text_bag, dtype=jnp.int32) // TEXT
    image_segs = jnp.sum(
        (jnp.arange(image_bag, dtype=jnp.int32)[:, None] >= seg_ends[None, :]).astype(jnp.int32),
        axis=1,
    )
    seg_range = jnp.arange(seg_count, dtype=jnp.int32)
    text_local = lax.dynamic_slice_in_dim(text_segs, seq_index * text_dev, text_dev)
    image_local = lax.dynamic_slice_in_dim(image_segs, seq_index * image_dev, image_dev)
    text_pick = (text_local[:, None] == seg_range[None, :]).astype(jnp.float32)
    image_pick = (image_local[:, None] == seg_range[None, :]).astype(jnp.float32)
    text_hidden = modulate(
        text_rows,
        pick_rows(text_pick, modulation[:, 0, 0]),
        pick_rows(text_pick, modulation[:, 0, 1]),
    )
    image_hidden = modulate(
        image_rows,
        pick_rows(image_pick, modulation[:, 1, 0]),
        pick_rows(image_pick, modulation[:, 1, 1]),
    )
    store_rows = jnp.take(store_row, user_adapter, axis=0)
    owners = store_rows // store_size
    owner_match = owners == bag_index
    sending = jnp.any(owner_match, axis=1)
    slot_index = jnp.sum(jnp.where(owner_match, store_rows % store_size, 0), axis=1)
    down_send = jnp.where(
        sending[:, None, None, None],
        jnp.take(store_down, slot_index, axis=0),
        jnp.zeros((), jnp.bfloat16),
    )
    up_send = jnp.where(
        sending[:, None, None, None],
        jnp.take(store_up, slot_index, axis=0),
        jnp.zeros((), jnp.bfloat16),
    )
    down_recv, up_recv = (
        lax.all_to_all(down_send, "bag", split_axis=0, concat_axis=0, tiled=True),
        lax.all_to_all(up_send, "bag", split_axis=0, concat_axis=0, tiled=True),
    )
    my_owners = lax.dynamic_index_in_dim(owners, bag_index, 0, keepdims=False)
    down_users = jnp.take(down_recv, my_owners, axis=0)
    up_users = jnp.take(up_recv, my_owners, axis=0)
    text_all, image_all = (
        lax.all_gather(text_hidden, "seq", axis=0, tiled=True),
        lax.all_gather(image_hidden, "seq", axis=0, tiled=True),
    )
    text_part = part_ranks(text_all, down_users[:, 0], text_segs // 2, user_count)
    image_part = part_ranks(image_all, down_users[:, 1], image_segs // 2, user_count)
    text_cols, image_cols = (
        lax.all_gather(text_part, "seq", axis=0, tiled=True),
        lax.all_gather(image_part, "seq", axis=0, tiled=True),
    )
    text_rank_all = text_cols.T
    image_rank_all = image_cols.T
    text_parts = adapted(
        text_all, head_weight[0], text_rank_all, up_users[:, 0], text_segs // 2, norm_gain[0]
    )
    image_parts = adapted(
        image_all, head_weight[1], image_rank_all, up_users[:, 1], image_segs // 2, norm_gain[1]
    )
    joined = [
        jnp.transpose(jnp.concatenate([text_parts[which], image_parts[which]], axis=0), (1, 0, 2))
        for which in range(3)
    ]
    seg_all = jnp.concatenate([text_segs, image_segs], axis=0)

    def one_head(head_rows):
        return attend(head_rows[0], head_rows[1], head_rows[2], seg_all)

    outputs = lax.map(one_head, (joined[0], joined[1], joined[2]))
    heads_here = outputs.shape[0]
    outputs = jnp.transpose(outputs, (1, 0, 2)).reshape(text_bag + image_bag, heads_here * HEAD_DIM)
    text_out, image_out = (
        lax.all_to_all(outputs[:text_bag], "seq", split_axis=0, concat_axis=1, tiled=True),
        lax.all_to_all(outputs[text_bag:], "seq", split_axis=0, concat_axis=1, tiled=True),
    )
    return (text_out, image_out)


def solution(mesh):
    in_specs = (
        P(("bag", "seq"), None),
        P(("bag", "seq"), None),
        P("bag", None, None, None),
        P(None, None, "seq"),
        P(),
        P("bag", None, "seq", None),
        P("bag", None, None, "seq"),
        P(),
        P(),
        P("bag", None),
    )
    out_specs = (P(("bag", "seq"), None), P(("bag", "seq"), None))
    return jax.shard_map(body, mesh=mesh, in_specs=in_specs, out_specs=out_specs, check_vma=False)
```

profile of v0, /device:TPU:0, one launch (start us, length us, event | category | flops | bytes accessed | tf_op | source)
XLA Modules:
  0.0 189.1 jit_solution(12241190175673804232)
XLA Ops:
  7.3 1.2 convert_reduce_fusion.1
  8.5 1.2 fusion.38
  10.7 2.2 %fusion.64 = (f32[8,1,1,3072]{3,2,1,0:T(1,128)}, f32[8,1,1,3072]{3,2,1,0:T(1,128)S(1)}, f32[8,1,1,3072]{3,2,1,0:T(1,128)}, f32[8,1,1,3072]{3,2,1,0:T(1,128)}) fusion(f32[8,2,2,3072]{3,2,1,0:T(2,128)} %param.16), kind=kLoop, calls=%fused_computation.163 | loop fusion | bytes 786432 | tf_op jit(solution)/shard_map/slice | solution.py:111
  13.0 1.3 fusion.15
  14.4 2.0 %fusion.16 = bf16[32,3072]{1,0:T(8,128)(2,1)} fusion(f32[32,3072]{1,0:T(8,128)S(1)} %fusion.15, f32[8,1,1,3072]{3,2,1,0:T(1,128)} %get-tuple-element.146, s32[32]{0:T(128)S(1)} %dynamic_slice.30), kind=kOutput, calls=%fused_computation.34 | convolution fusion | flops 9634048 | bytes 688256 | tf_op jit(solution)/shard_map/dot_general | solution.py:50
  20.5 1.3 gather_fusion.1
  22.5 1.1 fusion.39
  24.4 5.2 %all-to-all-start = ((bf16[4,2,8,3072]{3,2,1,0:T(8,128)(2,1)}), bf16[4,2,8,3072]{3,2,1,0:T(8,128)(2,1)}, u32[]{:S(2)}, u32[]{:S(2)}) async-start(bf16[4,2,8,3072]{3,2,1,0:T(8,128)(2,1)} %copy.93), calls=%async_computation | async-start | bytes 786432 | tf_op jit(solution)/shard_map/all_to_all | solution.py:135
  30.1 1.5 fusion.13
  31.6 2.2 %fusion.14 = bf16[64,3072]{1,0:T(8,128)(2,1)} fusion(f32[64,3072]{1,0:T(8,128)S(1)} %fusion.13, f32[8,1,1,3072]{3,2,1,0:T(1,128)} %get-tuple-element.143, s32[64]{0:T(128)S(1)} %dynamic_slice.28), kind=kOutput, calls=%fused_computation.30 | convolution fusion | flops 19268096 | bytes 1278208 | tf_op jit(solution)/shard_map/dot_general | solution.py:50
  35.2 1.4 slice_bitcast_fusion.7
  37.1 1.3 compare_and_fusion.1
  38.4 4.5 %gather_fusion.3 = bf16[4,2,64,768]{3,2,1,0:T(8,128)(2,1)} fusion(bf16[32,2,64,768]{3,2,1,0:T(8,128)(2,1)} %param.20, s32[1024]{0:T(1024)} %copy-done.13), kind=kCustom, calls=%fused_computation.3 | custom fusion | bytes 1572880 | tf_op jit(solution)/shard_map/jit(_take)/gather | solution.py:131
  42.9 2.2 %select_select_fusion = bf16[4,2,64,768]{3,2,1,0:T(8,128)(2,1)} fusion(bf16[4,2,64,768]{3,2,1,0:T(8,128)(2,1)} %gather_fusion.3, pred[4]{0:T(512)(128)(4,1)S(1)} %copy-done.19, pred[4]{0:T(512)(128)(4,1)} %copy-done.15), kind=kLoop, calls=%fused_computation.50 | loop fusion | flops 786432 | bytes 1572872 | tf_op jit(solution)/shard_map/jit(_where)/select_n | solution.py:129
  45.1 4.2 %all-to-all-start.1 = ((bf16[4,2,64,768]{3,2,1,0:T(8,128)(2,1)}), bf16[4,2,64,768]{3,2,1,0:T(8,128)(2,1)}, u32[]{:S(2)}, u32[]{:S(2)}) async-start(bf16[4,2,64,768]{3,2,1,0:T(8,128)(2,1)} %select_select_fusion), calls=%async_computation.1 | async-start | bytes 1572864 | tf_op jit(solution)/shard_map/all_to_all | solution.py:136
  49.3 2.3 %gather_fusion.2 = bf16[4,2,8,3072]{3,2,1,0:T(8,128)(2,1)} fusion(bf16[4,2,8,3072]{3,2,1,0:T(8,128)(2,1)} %all-to-all-done, s32[1024]{0:T(1024)S(1)} %pad_clamp_fusion), kind=kCustom, calls=%fused_computation.2 | custom fusion | bytes 786448 | tf_op jit(solution)/shard_map/jit(_take)/gather | solution.py:139
  51.6 1.1 copy_select_fusion
  52.7 8.0 %all-to-all-done.1 = bf16[4,2,64,768]{3,2,1,0:T(8,128)(2,1)} async-done(((bf16[4,2,64,768]{3,2,1,0:T(8,128)(2,1)}), bf16[4,2,64,768]{3,2,1,0:T(8,128)(2,1)}, u32[]{:S(2)}, u32[]{:S(2)}) %all-to-all-start.1) | async-done | bytes 786464 | tf_op jit(solution)/shard_map/all_to_all | solution.py:136
  60.7 2.8 %gather_fusion.4 = bf16[4,2,64,768]{3,2,1,0:T(8,128)(2,1)} fusion(bf16[4,2,64,768]{3,2,1,0:T(8,128)(2,1)} %all-to-all-done.1, s32[1024]{0:T(1024)} %copy-done.14), kind=kCustom, calls=%fused_computation.4 | custom fusion | bytes 1572880 | tf_op jit(solution)/shard_map/jit(_take)/gather | solution.py:140
  63.5 1.3 broadcast_select_fusion
  64.8 0.9 fusion.63
  65.7 2.0 %fusion.30 = bf16[8,256]{1,0:T(8,128)(2,1)S(1)} fusion(bf16[256,3072]{1,0:T(8,128)(2,1)} %all-gather.5.cloned.1.call-done, bf16[4,2,8,3072]{3,2,0,1:T(8,128)(2,1)S(1)} %copy_select_fusion, f32[4,256]{1,0:T(4,128)S(1)} %fusion.49), kind=kOutput, calls=%fused_computation.44 | convolution fusion | flops 50345984 | bytes 1777664 | tf_op jit(solution)/shard_map/nd,urd->urn/dot_general | solution.py:54
  67.7 14.8 %all_gather.15 = bf16[64,256]{1,0:T(8,128)(2,1)S(1)} all-gather(bf16[8,256]{1,0:T(8,128)(2,1)S(1)} %fusion.30), channel_id=1, replica_groups=mesh['bag'=4,'seq'=8] {'seq'}, dimensions={0}, use_global_device_ids=true | all-gather | bytes 36864 | tf_op jit(solution)/shard_map/all_gather | solution.py:149
  83.2 4.2 %fusion.7 = f32[256,768]{1,0:T(8,128)S(1)} fusion(bf16[256,3072]{1,0:T(8,128)(2,1)} %all-gather.5.cloned.1.call-done, bf16[2,3072,768]{2,1,0:T(8,128)(2,1)} %param.17), kind=kOutput, calls=%fused_computation.21 | convolution fusion | flops 1207959552 | bytes 7077888 | tf_op jit(solution)/shard_map/dot_general | solution.py:62
  87.4 1.2 convolution_add_fusion.5
  88.6 2.3 %copy.98 = f32[256,768]{0,1:T(8,128)} copy(f32[256,768]{1,0:T(8,128)} %convolution_add_fusion.5) | data formatting | bytes 1572864 | tf_op jit(solution)/shard_map/add | solution.py:69
  90.9 1.1 fusion.62
  92.1 1.6 fusion.41
  93.7 1.5 multiply_convert_fusion.2
  95.2 3.1 %fusion.24 = bf16[8,512]{1,0:T(8,128)(2,1)S(1)} fusion(bf16[512,3072]{1,0:T(8,128)(2,1)} %all-gather.3.cloned.1.call-done, bf16[4,2,8,3072]{3,2,0,1:T(8,128)(2,1)S(1)} %copy_select_fusion, f32[4,512]{1,0:T(4,128)S(1)} %fusion.47), kind=kOutput, calls=%fused_computation.42 | convolution fusion | flops 100691968 | bytes 3358720 | tf_op jit(solution)/shard_map/nd,urd->urn/dot_general | solution.py:54
  98.3 14.2 %all_gather.13 = bf16[64,512]{1,0:T(8,128)(2,1)S(1)} all-gather(bf16[8,512]{1,0:T(8,128)(2,1)S(1)} %fusion.24), channel_id=1, replica_groups=mesh['bag'=4,'seq'=8] {'seq'}, dimensions={0}, use_global_device_ids=true | all-gather | bytes 73728 | tf_op jit(solution)/shard_map/all_gather | solution.py:148
  112.5 5.0 %fusion.9 = f32[512,768]{1,0:T(8,128)S(1)} fusion(bf16[512,3072]{1,0:T(8,128)(2,1)S(1)} %copy-done.3, bf16[2,3072,768]{2,1,0:T(8,128)(2,1)} %param.17), kind=kOutput, calls=%fused_computation.23 | convolution fusion | flops 2415919104 | bytes 9437184 | tf_op jit(solution)/shard_map/dot_general | solution.py:62
  117.6 1.6 convolution_add_fusion.4
  119.1 3.1 %copy.95 = f32[512,768]{0,1:T(8,128)} copy(f32[512,768]{1,0:T(8,128)} %convolution_add_fusion.4) | data formatting | bytes 3145728 | tf_op jit(solution)/shard_map/add | solution.py:69
  122.2 1.4 multiply_reduce_fusion
  123.6 1.1 fusion.40
  124.7 1.3 multiply_convert_fusion
  128.4 26.8 %while.23 = (s32[]{:T(128)}, bf16[2,768,128]{2,1,0:T(8,128)(2,1)}, bf16[2,768,128]{1,2,0:T(8,128)(2,1)}, s32[768]{0:T(1024)S(1)}, bf16[2,768,128]{1,2,0:T(8,128)...) while((s32[]{:T(128)}, bf16[2,768,128]{2,1,0:T(8,128)(2,1)}, ...), condition=%wide.wide.region_19.20_spmd, body=%wide.wide.region_14.19_spmd.sunk | while | flops 102465024 | bytes 5647666 | solution.py:168
  128.4 0.9 constant_dynamic-slice_fusion.10
  130.2 1.0 constant_dynamic-slice_fusion.11
  132.2 8.0 %while.24 = (s32[]{:T(128)}, bf16[3,256,128]{2,1,0:T(8,128)(2,1)}, s32[3,256]{1,0:T(4,128)S(1)}, s32[768]{0:T(1024)S(1)}, bf16[3,256,128]{2,1,0:T(8,128)(2,1)}, ...) while((s32[]{:T(128)}, bf16[3,256,128]{2,1,0:T(8,128)(2,1)}, ...), condition=%wide.region_18.18_spmd, body=%wide.region_15.17_spmd.sunk | while | flops 102465024 | bytes 2894953 | solution.py:42
  132.2 1.3 fusion.81
  133.8 1.0 fusion.83
  134.9 1.3 fusion.81
  136.5 1.0 fusion.83
  137.5 1.3 fusion.81
  139.1 1.0 fusion.83
  140.2 1.6 bitcast_dynamic-update-slice_fusion.3
  141.8 0.9 constant_dynamic-slice_fusion.10
  143.6 1.0 constant_dynamic-slice_fusion.11
  145.6 8.0 %while.24 = (s32[]{:T(128)}, bf16[3,256,128]{2,1,0:T(8,128)(2,1)}, s32[3,256]{1,0:T(4,128)S(1)}, s32[768]{0:T(1024)S(1)}, bf16[3,256,128]{2,1,0:T(8,128)(2,1)}, ...) while((s32[]{:T(128)}, bf16[3,256,128]{2,1,0:T(8,128)(2,1)}, ...), condition=%wide.region_18.18_spmd, body=%wide.region_15.17_spmd.sunk | while | flops 102465024 | bytes 2894953 | solution.py:42
  145.6 1.3 fusion.81
  147.3 1.0 fusion.83
  148.3 1.3 fusion.81
  149.9 1.0 fusion.83
  151.0 1.3 fusion.81
  152.5 1.0 fusion.83
  153.6 1.6 bitcast_dynamic-update-slice_fusion.3
  155.2 0.9 slice.123
  157.0 4.7 %all-to-all-start.3 = ((bf16[8,32,256]{2,1,0:T(8,128)(2,1)}), bf16[8,32,256]{2,1,0:T(8,128)(2,1)S(1)}, u32[]{:S(2)}, u32[]{:S(2)}) async-start(bf16[8,32,256]{2,1,0:T(8,128)(2,1)} %all_to_all.40), calls=%async_computation.3 | async-start | bytes 262144 | tf_op jit(solution)/shard_map/all_to_all | solution.py:173
  161.8 1.0 slice.122
  163.9 4.6 %all-to-all-done.3 = bf16[8,32,256]{2,1,0:T(8,128)(2,1)S(1)} async-done(((bf16[8,32,256]{2,1,0:T(8,128)(2,1)}), bf16[8,32,256]{2,1,0:T(8,128)(2,1)S(1)}, u32[]{:S(2)}, u32[]{:S(2)}) %all-to-all-start.3) | async-done | bytes 131104 | tf_op jit(solution)/shard_map/all_to_all | solution.py:173
  168.5 3.4 %all-to-all-start.2 = ((bf16[8,64,256]{2,1,0:T(8,128)(2,1)}), bf16[8,64,256]{2,1,0:T(8,128)(2,1)S(1)}, u32[]{:S(2)}, u32[]{:S(2)}) async-start(bf16[8,64,256]{2,1,0:T(8,128)(2,1)} %all_to_all.36), calls=%async_computation.2 | async-start | bytes 524288 | tf_op jit(solution)/shard_map/all_to_all | solution.py:172
  172.6 9.0 %all-to-all-done.2 = bf16[8,64,256]{2,1,0:T(8,128)(2,1)S(1)} async-done(((bf16[8,64,256]{2,1,0:T(8,128)(2,1)}), bf16[8,64,256]{2,1,0:T(8,128)(2,1)S(1)}, u32[]{:S(2)}, u32[]{:S(2)}) %all-to-all-start.2) | async-done | bytes 262176 | tf_op jit(solution)/shard_map/all_to_all | solution.py:172
  (124 shorter events, 21.2 us)
Async XLA Ops:
  7.2 13.4 %copy-start = (bf16[32,2,8,3072]{3,2,1,0:T(8,128)(2,1)S(1)}, bf16[32,2,8,3072]{3,2,1,0:T(8,128)(2,1)}, u32[]{:S(2)}) copy-start(bf16[32,2,8,3072]{3,2,1,0:T(8,128)(2,1)} %param.19) | copy-start | bytes 9437188
  7.2 12.0 %copy-start.9 = (s32[4,4]{1,0:T(4,128)S(1)}, s32[4,4]{1,0:T(4,128)}, u32[]{:S(2)}) copy-start(s32[4,4]{1,0:T(4,128)} %param.22) | copy-start | bytes 196
  7.2 11.2 %copy-start.1 = (s32[128]{0:T(128)S(1)}, s32[128]{0:T(128)}, u32[]{:S(2)}) copy-start(s32[128]{0:T(128)} %param.21) | copy-start | bytes 1540
  7.2 58.5 %all-gather.5.cloned.1.call-start = ((), (), s32[]{:S(2)}) async-start(), calls=%async_computation.5 | async-start | bytes 1769472 | tf_op jit(solution)/shard_map/all_gather | solution.py:143
  10.7 2.3 %copy-start.16 = (s32[256]{0:T(256)}, s32[256]{0:T(256)S(1)}, u32[]{:S(2)}) copy-start(s32[256]{0:T(256)S(1)} %convert_reduce_fusion.2) | copy-start | bytes 3076
  14.4 15.3 %copy-start.2 = (bf16[64,3072]{1,0:T(8,128)(2,1)S(1)}, bf16[64,3072]{1,0:T(8,128)(2,1)}, u32[]{:S(2)}) copy-start(bf16[64,3072]{1,0:T(8,128)(2,1)} %param.14) | copy-start | bytes 1179652
  19.9 13.9 %copy-start.15 = (pred[4]{0:T(512)(128)(4,1)}, pred[4]{0:T(512)(128)(4,1)S(1)}, u32[]{:S(2)}) copy-start(pred[4]{0:T(512)(128)(4,1)S(1)} %get-tuple-element.130) | copy-start | bytes 16
  20.0 0.5 copy-start.22
  20.5 13.3 %copy-start.13 = (s32[1024]{0:T(1024)}, s32[1024]{0:T(1024)S(1)}, u32[]{:S(2)}) copy-start(s32[1024]{0:T(1024)S(1)} %pad_clamp_fusion.1) | copy-start | bytes 12292
  21.9 12.0 %copy-start.17 = (s32[256]{0:T(256)S(1)}, s32[256]{0:T(256)}, u32[]{:S(2)}) copy-start(s32[256]{0:T(256)} %copy-done.16) | copy-start | bytes 3076
  22.5 7.1 %copy-start.18 = (pred[4]{0:T(512)(128)(4,1)}, pred[4]{0:T(512)(128)(4,1)S(1)}, u32[]{:S(2)}) copy-start(pred[4]{0:T(512)(128)(4,1)S(1)} %compare_and_fusion) | copy-start | bytes 16
  24.4 20.7 %all-to-all-start = ((bf16[4,2,8,3072]{3,2,1,0:T(8,128)(2,1)}), bf16[4,2,8,3072]{3,2,1,0:T(8,128)(2,1)}, u32[]{:S(2)}, u32[]{:S(2)}) async-start(bf16[4,2,8,3072]{3,2,1,0:T(8,128)(2,1)} %copy.93), calls=%async_computation | async-start | bytes 786432 | tf_op jit(solution)/shard_map/all_to_all | solution.py:135
  29.6 65.6 %all-gather.3.cloned.1.call-start = ((), (), s32[]{:S(2)}) async-start(), calls=%async_computation.4 | async-start | bytes 3538944 | tf_op jit(solution)/shard_map/all_gather | solution.py:142
  31.6 11.3 %copy-start.19 = (pred[4]{0:T(512)(128)(4,1)S(1)}, pred[4]{0:T(512)(128)(4,1)}, u32[]{:S(2)}) copy-start(pred[4]{0:T(512)(128)(4,1)} %copy-done.18) | copy-start | bytes 16
  33.9 15.4 %copy-start.10 = (s32[768]{0:T(1024)}, s32[768]{0:T(1024)S(1)}, u32[]{:S(2)}) copy-start(s32[768]{0:T(1024)S(1)} %pad_add_fusion) | copy-start | bytes 9220
  34.6 14.7 %copy-start.14 = (s32[1024]{0:T(1024)}, s32[1024]{0:T(1024)S(1)}, u32[]{:S(2)}) copy-start(s32[1024]{0:T(1024)S(1)} %pad_clamp_fusion) | copy-start | bytes 12292
  45.1 15.6 %all-to-all-start.1 = ((bf16[4,2,64,768]{3,2,1,0:T(8,128)(2,1)}), bf16[4,2,64,768]{3,2,1,0:T(8,128)(2,1)}, u32[]{:S(2)}, u32[]{:S(2)}) async-start(bf16[4,2,64,768]{3,2,1,0:T(8,128)(2,1)} %select_select_fusion), calls=%async_computation.1 | async-start | bytes 1572864 | tf_op jit(solution)/shard_map/all_to_all | solution.py:136
  83.2 4.3 %copy-start.5 = (bf16[4,1,64,768]{3,2,1,0:T(8,128)(2,1)S(1)}, bf16[4,1,64,768]{3,2,1,0:T(8,128)(2,1)}, u32[]{:S(2)}) copy-start(bf16[4,1,64,768]{3,2,1,0:T(8,128)(2,1)} %get-tuple-element.142) | copy-start | bytes 1179652
  90.9 21.6 %copy-start.12 = (bf16[512,4]{0,1:T(4,128)(2,1)S(1)}, bf16[512,4]{0,1:T(4,128)(2,1)}, u32[]{:S(2)}) copy-start(bf16[512,4]{0,1:T(4,128)(2,1)} %fusion.46) | copy-start | bytes 12292
  95.2 17.3 %copy-start.3 = (bf16[512,3072]{1,0:T(8,128)(2,1)S(1)}, bf16[512,3072]{1,0:T(8,128)(2,1)}, u32[]{:S(2)}) copy-start(bf16[512,3072]{1,0:T(8,128)(2,1)} %all-gather.3.cloned.1.call-done) | copy-start | bytes 9437188
  112.5 5.0 %copy-start.4 = (bf16[4,1,64,768]{3,2,1,0:T(8,128)(2,1)S(1)}, bf16[4,1,64,768]{3,2,1,0:T(8,128)(2,1)}, u32[]{:S(2)}) copy-start(bf16[4,1,64,768]{3,2,1,0:T(8,128)(2,1)} %get-tuple-element.141) | copy-start | bytes 1179652
  119.1 5.6 %copy-start.20 = (f32[128]{0:T(128)S(1)}, f32[128]{0:T(128)}, u32[]{:S(2)}) copy-start(f32[128]{0:T(128)} %get-tuple-element.147) | copy-start | bytes 1540
  119.1 5.6 %copy-start.21 = (f32[128]{0:T(128)S(1)}, f32[128]{0:T(128)}, u32[]{:S(2)}) copy-start(f32[128]{0:T(128)} %get-tuple-element.149) | copy-start | bytes 1540
  119.1 6.9 %copy-start.8 = (bf16[256,2,128]{0,2,1:T(8,128)(2,1)S(1)}, bf16[256,2,128]{0,2,1:T(8,128)(2,1)}, u32[]{:S(2)}) copy-start(bf16[256,2,128]{0,2,1:T(8,128)(2,1)} %get-tuple-element.151) | copy-start | bytes 393220
  119.1 7.7 %copy-start.6 = (bf16[256,2,128]{0,2,1:T(8,128)(2,1)S(1)}, bf16[256,2,128]{0,2,1:T(8,128)(2,1)}, u32[]{:S(2)}) copy-start(bf16[256,2,128]{0,2,1:T(8,128)(2,1)} %fusion.41) | copy-start | bytes 393220
  122.2 5.4 %copy-start.7 = (bf16[256,2,128]{0,2,1:T(8,128)(2,1)S(1)}, bf16[256,2,128]{0,2,1:T(8,128)(2,1)}, u32[]{:S(2)}) copy-start(bf16[256,2,128]{0,2,1:T(8,128)(2,1)} %get-tuple-element.152) | copy-start | bytes 393220
  122.2 6.2 %copy-start.11 = (s32[768]{0:T(1024)S(1)}, s32[768]{0:T(1024)}, u32[]{:S(2)}) copy-start(s32[768]{0:T(1024)} %copy-done.10) | copy-start | bytes 9220
  157.0 11.5 %all-to-all-start.3 = ((bf16[8,32,256]{2,1,0:T(8,128)(2,1)}), bf16[8,32,256]{2,1,0:T(8,128)(2,1)S(1)}, u32[]{:S(2)}, u32[]{:S(2)}) async-start(bf16[8,32,256]{2,1,0:T(8,128)(2,1)} %all_to_all.40), calls=%async_computation.3 | async-start | bytes 262144 | tf_op jit(solution)/shard_map/all_to_all | solution.py:173
  168.5 13.1 %all-to-all-start.2 = ((bf16[8,64,256]{2,1,0:T(8,128)(2,1)}), bf16[8,64,256]{2,1,0:T(8,128)(2,1)S(1)}, u32[]{:S(2)}, u32[]{:S(2)}) async-start(bf16[8,64,256]{2,1,0:T(8,128)(2,1)} %all_to_all.36), calls=%async_computation.2 | async-start | bytes 524288 | tf_op jit(solution)/shard_map/all_to_all | solution.py:172
Sparse Core Ops, SparseCore 0:
  16.5 27.9 all-gather.4
  46.2 37.7 all-gather.2
where the time goes:
time: 191 us; the launch traced here: 189 us
  local copies, waits for them, and re-layouts  44.5 us (23%)
  matrix products  38.2 us (20%)
  blocking collectives  29 us (15%)
  other arithmetic  23.8 us (12%)
  waiting for transfers between devices  21.6 us (11%)
  starting transfers between devices  17.6 us (9%)
  between operations  14.4 us (8%)
    all_gather x1, blocking collectives, body(): lax.all_gather(image_part, 'seq', axis=0, tiled=True)  14.8 us
    all_gather x1, blocking collectives, body(): lax.all_gather(text_part, 'seq', axis=0, tiled=True)  14.2 us
    dot_general x2, matrix products, adapted(): plain_part = jnp.dot(hidden_all, weight, preferred_element_type=jnp.float32)  9.25 us
    all_to_all x1, waiting for transfers between devices, body(): lax.all_to_all(outputs[:text_bag], 'seq', split_axis=0, concat_axis=1, ti...  8.97 us
    all_to_all x1, waiting for transfers between devices, body(): lax.all_to_all(up_send, 'bag', split_axis=0, concat_axis=0, tiled=True)  7.96 us
    dot_general x6, matrix products, one_block(): jnp.dot(query_rows, keys_all.T, preferred_element_type=jnp.float32) * factor  7.93 us
    dynamic_slice x10, local copies, waits for them, and re-layouts, body(): outputs = lax.map(one_head, (joined[0], joined[1], joined[2]))  7.58 us
    dot_general x4, matrix products, pick_rows(): return jnp.dot(seg_pick, table_rows, precision=lax.Precision.HIGHEST)  6.94 us
  transfers between devices with their start and end apart: 6, of which 3 were waited for; matrix products, arithmetic and copies ran while one was open for 25% of the time, Pallas kernels for 0%

commit v1 on v0

--- a/solution.py
+++ b/solution.py
@@ -169,7 +169,12 @@
     heads_here = outputs.shape[0]
     outputs = jnp.transpose(outputs, (1, 0, 2)).reshape(text_bag + image_bag, heads_here * HEAD_DIM)
     text_out, image_out = (
-        lax.all_to_all(outputs[:text_bag], "seq", split_axis=0, concat_axis=1, tiled=True),
+        jnp.concatenate(
+            lax.all_to_all(
+                jnp.stack(jnp.split(outputs[:text_bag], lax.axis_size("seq"), axis=0)), "seq", 0, 0
+            ),
+            axis=1,
+        ),
         lax.all_to_all(outputs[text_bag:], "seq", split_axis=0, concat_axis=1, tiled=True),
     )
     return (text_out, image_out)

time: 191 us -> 206 us (1.079)
  local copies, waits for them, and re-layouts: 44.5 us -> 61.8 us
  waiting for transfers between devices: 21.6 us -> 17 us
    another operation x1 -> x10, local copies, waits for them, and re-layouts: 0.08 us -> 7.45 us  [the longest x9 7.36 us: body(): jnp.stack(jnp.split(outputs[:text_bag], lax.axis_size('seq'), axis=0))]
    split x0 -> x9, local copies, waits for them, and re-layouts: none -> 6.06 us  [body(): jnp.split(outputs[:text_bag], lax.axis_size('seq'), axis=0)]
    unnamed x46 -> x55, local copies, waits for them, and re-layouts: 0.6 us -> 6.64 us
    all_to_all x1, waiting for transfers between devices: 4.63 us -> 0.01 us  [body(): lax.all_to_all(outputs[text_bag:], 'seq', split_axis=0, concat_axis=1, ti...]
  transfers between devices with their start and end apart: 6 -> 6, of which waited for: 3 -> 2; matrix products, arithmetic and copies ran while one was open for 25% -> 31% of each run, Pallas kernels for 0% -> 0%
where the time goes in v1:
time: 206 us; the launch traced here: 203 us
  local copies, waits for them, and re-layouts  61.8 us (30%)
  matrix products  38.2 us (19%)
  blocking collectives  29.1 us (14%)
  other arithmetic  23.8 us (12%)
  starting transfers between devices  19.2 us (9%)
  waiting for transfers between devices  17 us (8%)
  between operations  14.4 us (7%)
    all_gather x1, blocking collectives, body(): lax.all_gather(image_part, 'seq', axis=0, tiled=True)  14.9 us
    all_gather x1, blocking collectives, body(): lax.all_gather(text_part, 'seq', axis=0, tiled=True)  14.2 us
    dot_general x2, matrix products, adapted(): plain_part = jnp.dot(hidden_all, weight, preferred_element_type=jnp.float32)  9.24 us
    all_to_all x1, waiting for transfers between devices, body(): lax.all_to_all(jnp.stack(jnp.split(outputs[:text_bag], lax.axis_size('seq...  9.05 us
    all_to_all x1, waiting for transfers between devices, body(): lax.all_to_all(up_send, 'bag', split_axis=0, concat_axis=0, tiled=True)  7.95 us
    dot_general x6, matrix products, one_block(): jnp.dot(query_rows, keys_all.T, preferred_element_type=jnp.float32) * factor  7.93 us
    dynamic_slice x10, local copies, waits for them, and re-layouts, body(): outputs = lax.map(one_head, (joined[0], joined[1], joined[2]))  7.58 us
    another operation x9, local copies, waits for them, and re-layouts, body(): jnp.stack(jnp.split(outputs[:text_bag], lax.axis_size('seq'), axis=0))  7.36 us
  transfers between devices with their start and end apart: 6, of which 2 were waited for; matrix products, arithmetic and copies ran while one was open for 31% of the time, Pallas kernels for 0%

profile of v1, /device:TPU:0, one launch (start us, length us, event | category | flops | bytes accessed | tf_op | source)
XLA Modules:
  0.0 203.5 jit_solution(13947096180868856419)
XLA Ops:
  7.3 1.2 convert_reduce_fusion.1
  8.5 1.2 fusion.38
  10.7 2.2 %fusion.65 = (f32[8,1,1,3072]{3,2,1,0:T(1,128)}, f32[8,1,1,3072]{3,2,1,0:T(1,128)S(1)}, f32[8,1,1,3072]{3,2,1,0:T(1,128)}, f32[8,1,1,3072]{3,2,1,0:T(1,128)}) fusion(f32[8,2,2,3072]{3,2,1,0:T(2,128)} %param.16), kind=kLoop, calls=%fused_computation.172 | loop fusion | bytes 786432 | tf_op jit(solution)/shard_map/slice | solution.py:111
  13.1 1.3 fusion.15
  14.4 2.0 fusion.16
  20.4 1.3 gather_fusion.1
  22.4 1.1 fusion.39
  24.3 5.2 %all-to-all-start = ((bf16[4,2,8,3072]{3,2,1,0:T(8,128)(2,1)}), bf16[4,2,8,3072]{3,2,1,0:T(8,128)(2,1)}, u32[]{:S(2)}, u32[]{:S(2)}) async-start(bf16[4,2,8,3072]{3,2,1,0:T(8,128)(2,1)} %copy.121), calls=%async_computation | async-start | bytes 786432 | tf_op jit(solution)/shard_map/all_to_all | solution.py:135
  30.0 1.5 fusion.13
  31.5 2.2 %fusion.14 = bf16[64,3072]{1,0:T(8,128)(2,1)} fusion(f32[64,3072]{1,0:T(8,128)S(1)} %fusion.13, f32[8,1,1,3072]{3,2,1,0:T(1,128)} %get-tuple-element.151, s32[64]{0:T(128)S(1)} %dynamic_slice.28), kind=kOutput, calls=%fused_computation.30 | convolution fusion | flops 19268096 | bytes 1278208 | tf_op jit(solution)/shard_map/dot_general | solution.py:50
  35.1 1.4 slice_bitcast_fusion.7
  37.0 1.3 compare_and_fusion.1
  38.3 4.5 %gather_fusion.3 = bf16[4,2,64,768]{3,2,1,0:T(8,128)(2,1)} fusion(bf16[32,2,64,768]{3,2,1,0:T(8,128)(2,1)} %param.20, s32[1024]{0:T(1024)} %copy-done.14), kind=kCustom, calls=%fused_computation.3 | custom fusion | bytes 1572880 | tf_op jit(solution)/shard_map/jit(_take)/gather | solution.py:131
  42.8 2.2 %select_select_fusion = bf16[4,2,64,768]{3,2,1,0:T(8,128)(2,1)} fusion(bf16[4,2,64,768]{3,2,1,0:T(8,128)(2,1)} %gather_fusion.3, pred[4]{0:T(512)(128)(4,1)S(1)} %copy-done.20, pred[4]{0:T(512)(128)(4,1)} %copy-done.16), kind=kLoop, calls=%fused_computation.50 | loop fusion | flops 786432 | bytes 1572872 | tf_op jit(solution)/shard_map/jit(_where)/select_n | solution.py:129
  45.0 4.2 %all-to-all-start.1 = ((bf16[4,2,64,768]{3,2,1,0:T(8,128)(2,1)}), bf16[4,2,64,768]{3,2,1,0:T(8,128)(2,1)}, u32[]{:S(2)}, u32[]{:S(2)}) async-start(bf16[4,2,64,768]{3,2,1,0:T(8,128)(2,1)} %select_select_fusion), calls=%async_computation.1 | async-start | bytes 1572864 | tf_op jit(solution)/shard_map/all_to_all | solution.py:136
  49.2 2.3 %gather_fusion.2 = bf16[4,2,8,3072]{3,2,1,0:T(8,128)(2,1)} fusion(bf16[4,2,8,3072]{3,2,1,0:T(8,128)(2,1)} %all-to-all-done, s32[1024]{0:T(1024)S(1)} %pad_clamp_fusion), kind=kCustom, calls=%fused_computation.2 | custom fusion | bytes 786448 | tf_op jit(solution)/shard_map/jit(_take)/gather | solution.py:139
  51.5 1.1 copy_select_fusion
  52.6 7.9 %all-to-all-done.1 = bf16[4,2,64,768]{3,2,1,0:T(8,128)(2,1)} async-done(((bf16[4,2,64,768]{3,2,1,0:T(8,128)(2,1)}), bf16[4,2,64,768]{3,2,1,0:T(8,128)(2,1)}, u32[]{:S(2)}, u32[]{:S(2)}) %all-to-all-start.1) | async-done | bytes 786464 | tf_op jit(solution)/shard_map/all_to_all | solution.py:136
  60.6 2.8 %gather_fusion.4 = bf16[4,2,64,768]{3,2,1,0:T(8,128)(2,1)} fusion(bf16[4,2,64,768]{3,2,1,0:T(8,128)(2,1)} %all-to-all-done.1, s32[1024]{0:T(1024)} %copy-done.15), kind=kCustom, calls=%fused_computation.4 | custom fusion | bytes 1572880 | tf_op jit(solution)/shard_map/jit(_take)/gather | solution.py:140
  63.4 1.3 broadcast_select_fusion
  64.6 1.0 fusion.63
  65.6 2.0 fusion.30
  67.6 14.9 %all_gather.15 = bf16[64,256]{1,0:T(8,128)(2,1)S(1)} all-gather(bf16[8,256]{1,0:T(8,128)(2,1)S(1)} %fusion.30), channel_id=1, replica_groups=mesh['bag'=4,'seq'=8] {'seq'}, dimensions={0}, use_global_device_ids=true | all-gather | bytes 36864 | tf_op jit(solution)/shard_map/all_gather | solution.py:149
  83.2 4.2 %fusion.7 = f32[256,768]{1,0:T(8,128)S(1)} fusion(bf16[256,3072]{1,0:T(8,128)(2,1)} %all-gather.5.cloned.1.call-done, bf16[2,3072,768]{2,1,0:T(8,128)(2,1)} %param.17), kind=kOutput, calls=%fused_computation.21 | convolution fusion | flops 1207959552 | bytes 7077888 | tf_op jit(solution)/shard_map/dot_general | solution.py:62
  87.4 1.2 convolution_add_fusion.5
  88.6 2.3 %copy.126 = f32[256,768]{0,1:T(8,128)} copy(f32[256,768]{1,0:T(8,128)} %convolution_add_fusion.5) | data formatting | bytes 1572864 | tf_op jit(solution)/shard_map/add | solution.py:69
  90.9 1.1 fusion.62
  92.1 1.6 fusion.41
  93.7 1.5 multiply_convert_fusion.2
  95.2 3.1 %fusion.24 = bf16[8,512]{1,0:T(8,128)(2,1)S(1)} fusion(bf16[512,3072]{1,0:T(8,128)(2,1)} %all-gather.3.cloned.1.call-done, bf16[4,2,8,3072]{3,2,0,1:T(8,128)(2,1)S(1)} %copy_select_fusion, f32[4,512]{1,0:T(4,128)S(1)} %fusion.47), kind=kOutput, calls=%fused_computation.42 | convolution fusion | flops 100691968 | bytes 3358720 | tf_op jit(solution)/shard_map/nd,urd->urn/dot_general | solution.py:54
  98.3 14.2 %all_gather.13 = bf16[64,512]{1,0:T(8,128)(2,1)S(1)} all-gather(bf16[8,512]{1,0:T(8,128)(2,1)S(1)} %fusion.24), channel_id=1, replica_groups=mesh['bag'=4,'seq'=8] {'seq'}, dimensions={0}, use_global_device_ids=true | all-gather | bytes 73728 | tf_op jit(solution)/shard_map/all_gather | solution.py:148
  112.5 5.0 %fusion.9 = f32[512,768]{1,0:T(8,128)S(1)} fusion(bf16[512,3072]{1,0:T(8,128)(2,1)S(1)} %copy-done.3, bf16[2,3072,768]{2,1,0:T(8,128)(2,1)} %param.17), kind=kOutput, calls=%fused_computation.23 | convolution fusion | flops 2415919104 | bytes 9437184 | tf_op jit(solution)/shard_map/dot_general | solution.py:62
  117.5 1.6 convolution_add_fusion.4
  119.1 3.1 %copy.123 = f32[512,768]{0,1:T(8,128)} copy(f32[512,768]{1,0:T(8,128)} %convolution_add_fusion.4) | data formatting | bytes 3145728 | tf_op jit(solution)/shard_map/add | solution.py:69
  122.2 1.4 multiply_reduce_fusion
  123.6 1.1 fusion.40
  124.7 1.3 multiply_convert_fusion
  128.4 26.8 %while.23 = (s32[]{:T(128)}, bf16[2,768,128]{2,1,0:T(8,128)(2,1)}, bf16[2,768,128]{1,2,0:T(8,128)(2,1)}, s32[768]{0:T(1024)S(1)}, bf16[2,768,128]{1,2,0:T(8,128)...) while((s32[]{:T(128)}, bf16[2,768,128]{2,1,0:T(8,128)(2,1)}, ...), condition=%wide.wide.region_19.20_spmd, body=%wide.wide.region_14.19_spmd.sunk | while | flops 102465024 | bytes 5647666 | solution.py:168
  130.1 1.0 constant_dynamic-slice_fusion.11
  132.2 8.0 %while.24 = (s32[]{:T(128)}, bf16[3,256,128]{2,1,0:T(8,128)(2,1)}, s32[3,256]{1,0:T(4,128)S(1)}, s32[768]{0:T(1024)S(1)}, bf16[3,256,128]{2,1,0:T(8,128)(2,1)}, ...) while((s32[]{:T(128)}, bf16[3,256,128]{2,1,0:T(8,128)(2,1)}, ...), condition=%wide.region_18.18_spmd, body=%wide.region_15.17_spmd.sunk | while | flops 102465024 | bytes 2894953 | solution.py:42
  132.2 1.3 fusion.82
  133.8 1.0 fusion.84
  134.9 1.3 fusion.82
  136.5 1.0 fusion.84
  137.5 1.3 fusion.82
  139.1 1.0 fusion.84
  140.1 1.6 bitcast_dynamic-update-slice_fusion.3
  143.5 1.0 constant_dynamic-slice_fusion.11
  145.6 8.0 %while.24 = (s32[]{:T(128)}, bf16[3,256,128]{2,1,0:T(8,128)(2,1)}, s32[3,256]{1,0:T(4,128)S(1)}, s32[768]{0:T(1024)S(1)}, bf16[3,256,128]{2,1,0:T(8,128)(2,1)}, ...) while((s32[]{:T(128)}, bf16[3,256,128]{2,1,0:T(8,128)(2,1)}, ...), condition=%wide.region_18.18_spmd, body=%wide.region_15.17_spmd.sunk | while | flops 102465024 | bytes 2894953 | solution.py:42
  145.6 1.3 fusion.82
  147.2 1.0 fusion.84
  148.3 1.3 fusion.82
  149.9 1.0 fusion.84
  150.9 1.3 fusion.82
  152.5 1.0 fusion.84
  153.6 1.6 bitcast_dynamic-update-slice_fusion.3
  156.1 1.5 fusion.64
  158.5 4.7 %all-to-all-start.3 = ((bf16[8,32,256]{2,1,0:T(8,128)(2,1)}), bf16[8,32,256]{2,1,0:T(8,128)(2,1)S(1)}, u32[]{:S(2)}, u32[]{:S(2)}) async-start(bf16[8,32,256]{2,1,0:T(8,128)(2,1)} %all_to_all.26), calls=%async_computation.3 | async-start | bytes 262144 | tf_op jit(solution)/shard_map/all_to_all | solution.py:178
  173.3 1.4 copy.140
  174.7 1.4 stack.34
  176.1 1.4 copy.139
  177.5 1.4 stack.33
  181.1 5.1 %all-to-all-start.2 = ((bf16[8,64,256]{2,1,0:T(8,128)(2,1)}), bf16[8,64,256]{2,1,0:T(8,128)(2,1)S(1)}, u32[]{:S(2)}, u32[]{:S(2)}) async-start(bf16[8,64,256]{2,1,0:T(8,128)(2,1)} %copy-done.9), calls=%async_computation.2 | async-start | bytes 524288 | tf_op jit(solution)/shard_map/all_to_all | solution.py:173
  186.9 9.0 %all-to-all-done.2 = bf16[8,64,256]{2,1,0:T(8,128)(2,1)S(1)} async-done(((bf16[8,64,256]{2,1,0:T(8,128)(2,1)}), bf16[8,64,256]{2,1,0:T(8,128)(2,1)S(1)}, u32[]{:S(2)}, u32[]{:S(2)}) %all-to-all-start.2) | async-done | bytes 262176 | tf_op jit(solution)/shard_map/all_to_all | solution.py:173
  (148 shorter events, 35.1 us)
Async XLA Ops:
  7.2 13.2 %copy-start = (bf16[32,2,8,3072]{3,2,1,0:T(8,128)(2,1)S(1)}, bf16[32,2,8,3072]{3,2,1,0:T(8,128)(2,1)}, u32[]{:S(2)}) copy-start(bf16[32,2,8,3072]{3,2,1,0:T(8,128)(2,1)} %param.19) | copy-start | bytes 9437188
  7.2 11.8 %copy-start.10 = (s32[4,4]{1,0:T(4,128)S(1)}, s32[4,4]{1,0:T(4,128)}, u32[]{:S(2)}) copy-start(s32[4,4]{1,0:T(4,128)} %param.22) | copy-start | bytes 196
  7.2 11.1 %copy-start.1 = (s32[128]{0:T(128)S(1)}, s32[128]{0:T(128)}, u32[]{:S(2)}) copy-start(s32[128]{0:T(128)} %param.21) | copy-start | bytes 1540
  7.2 58.4 %all-gather.5.cloned.1.call-start = ((), (), s32[]{:S(2)}) async-start(), calls=%async_computation.5 | async-start | bytes 1769472 | tf_op jit(solution)/shard_map/all_gather | solution.py:143
  10.7 2.3 %copy-start.17 = (s32[256]{0:T(256)}, s32[256]{0:T(256)S(1)}, u32[]{:S(2)}) copy-start(s32[256]{0:T(256)S(1)} %convert_reduce_fusion.2) | copy-start | bytes 3076
  14.4 15.2 %copy-start.2 = (bf16[64,3072]{1,0:T(8,128)(2,1)S(1)}, bf16[64,3072]{1,0:T(8,128)(2,1)}, u32[]{:S(2)}) copy-start(bf16[64,3072]{1,0:T(8,128)(2,1)} %param.14) | copy-start | bytes 1179652
  19.7 13.9 %copy-start.16 = (pred[4]{0:T(512)(128)(4,1)}, pred[4]{0:T(512)(128)(4,1)S(1)}, u32[]{:S(2)}) copy-start(pred[4]{0:T(512)(128)(4,1)S(1)} %get-tuple-element.130) | copy-start | bytes 16
  19.9 0.5 copy-start.23
  20.4 13.3 %copy-start.14 = (s32[1024]{0:T(1024)}, s32[1024]{0:T(1024)S(1)}, u32[]{:S(2)}) copy-start(s32[1024]{0:T(1024)S(1)} %pad_clamp_fusion.1) | copy-start | bytes 12292
  21.7 12.0 %copy-start.18 = (s32[256]{0:T(256)S(1)}, s32[256]{0:T(256)}, u32[]{:S(2)}) copy-start(s32[256]{0:T(256)} %copy-done.17) | copy-start | bytes 3076
  22.4 7.1 %copy-start.19 = (pred[4]{0:T(512)(128)(4,1)}, pred[4]{0:T(512)(128)(4,1)S(1)}, u32[]{:S(2)}) copy-start(pred[4]{0:T(512)(128)(4,1)S(1)} %compare_and_fusion) | copy-start | bytes 16
  24.3 20.7 %all-to-all-start = ((bf16[4,2,8,3072]{3,2,1,0:T(8,128)(2,1)}), bf16[4,2,8,3072]{3,2,1,0:T(8,128)(2,1)}, u32[]{:S(2)}, u32[]{:S(2)}) async-start(bf16[4,2,8,3072]{3,2,1,0:T(8,128)(2,1)} %copy.121), calls=%async_computation | async-start | bytes 786432 | tf_op jit(solution)/shard_map/all_to_all | solution.py:135
  29.5 65.7 %all-gather.3.cloned.1.call-start = ((), (), s32[]{:S(2)}) async-start(), calls=%async_computation.4 | async-start | bytes 3538944 | tf_op jit(solution)/shard_map/all_gather | solution.py:142
  31.5 11.3 %copy-start.20 = (pred[4]{0:T(512)(128)(4,1)S(1)}, pred[4]{0:T(512)(128)(4,1)}, u32[]{:S(2)}) copy-start(pred[4]{0:T(512)(128)(4,1)} %copy-done.19) | copy-start | bytes 16
  33.8 15.4 %copy-start.11 = (s32[768]{0:T(1024)}, s32[768]{0:T(1024)S(1)}, u32[]{:S(2)}) copy-start(s32[768]{0:T(1024)S(1)} %pad_add_fusion) | copy-start | bytes 9220
  34.5 14.8 %copy-start.15 = (s32[1024]{0:T(1024)}, s32[1024]{0:T(1024)S(1)}, u32[]{:S(2)}) copy-start(s32[1024]{0:T(1024)S(1)} %pad_clamp_fusion) | copy-start | bytes 12292
  45.0 15.6 %all-to-all-start.1 = ((bf16[4,2,64,768]{3,2,1,0:T(8,128)(2,1)}), bf16[4,2,64,768]{3,2,1,0:T(8,128)(2,1)}, u32[]{:S(2)}, u32[]{:S(2)}) async-start(bf16[4,2,64,768]{3,2,1,0:T(8,128)(2,1)} %select_select_fusion), calls=%async_computation.1 | async-start | bytes 1572864 | tf_op jit(solution)/shard_map/all_to_all | solution.py:136
  83.2 4.3 %copy-start.5 = (bf16[4,1,64,768]{3,2,1,0:T(8,128)(2,1)S(1)}, bf16[4,1,64,768]{3,2,1,0:T(8,128)(2,1)}, u32[]{:S(2)}) copy-start(bf16[4,1,64,768]{3,2,1,0:T(8,128)(2,1)} %get-tuple-element.142) | copy-start | bytes 1179652
  90.9 21.5 %copy-start.13 = (bf16[512,4]{0,1:T(4,128)(2,1)S(1)}, bf16[512,4]{0,1:T(4,128)(2,1)}, u32[]{:S(2)}) copy-start(bf16[512,4]{0,1:T(4,128)(2,1)} %fusion.46) | copy-start | bytes 12292
  95.2 17.3 %copy-start.3 = (bf16[512,3072]{1,0:T(8,128)(2,1)S(1)}, bf16[512,3072]{1,0:T(8,128)(2,1)}, u32[]{:S(2)}) copy-start(bf16[512,3072]{1,0:T(8,128)(2,1)} %all-gather.3.cloned.1.call-done) | copy-start | bytes 9437188
  112.5 5.0 %copy-start.4 = (bf16[4,1,64,768]{3,2,1,0:T(8,128)(2,1)S(1)}, bf16[4,1,64,768]{3,2,1,0:T(8,128)(2,1)}, u32[]{:S(2)}) copy-start(bf16[4,1,64,768]{3,2,1,0:T(8,128)(2,1)} %get-tuple-element.141) | copy-start | bytes 1179652
  119.1 5.6 %copy-start.21 = (f32[128]{0:T(128)S(1)}, f32[128]{0:T(128)}, u32[]{:S(2)}) copy-start(f32[128]{0:T(128)} %get-tuple-element.155) | copy-start | bytes 1540
  119.1 5.6 %copy-start.22 = (f32[128]{0:T(128)S(1)}, f32[128]{0:T(128)}, u32[]{:S(2)}) copy-start(f32[128]{0:T(128)} %get-tuple-element.157) | copy-start | bytes 1540
  119.1 6.9 %copy-start.8 = (bf16[256,2,128]{0,2,1:T(8,128)(2,1)S(1)}, bf16[256,2,128]{0,2,1:T(8,128)(2,1)}, u32[]{:S(2)}) copy-start(bf16[256,2,128]{0,2,1:T(8,128)(2,1)} %get-tuple-element.159) | copy-start | bytes 393220
  119.1 7.7 %copy-start.6 = (bf16[256,2,128]{0,2,1:T(8,128)(2,1)S(1)}, bf16[256,2,128]{0,2,1:T(8,128)(2,1)}, u32[]{:S(2)}) copy-start(bf16[256,2,128]{0,2,1:T(8,128)(2,1)} %fusion.41) | copy-start | bytes 393220
  122.2 5.4 %copy-start.7 = (bf16[256,2,128]{0,2,1:T(8,128)(2,1)S(1)}, bf16[256,2,128]{0,2,1:T(8,128)(2,1)}, u32[]{:S(2)}) copy-start(bf16[256,2,128]{0,2,1:T(8,128)(2,1)} %get-tuple-element.160) | copy-start | bytes 393220
  122.2 6.2 %copy-start.12 = (s32[768]{0:T(1024)S(1)}, s32[768]{0:T(1024)}, u32[]{:S(2)}) copy-start(s32[768]{0:T(1024)} %copy-done.11) | copy-start | bytes 9220
  158.5 22.6 %all-to-all-start.3 = ((bf16[8,32,256]{2,1,0:T(8,128)(2,1)}), bf16[8,32,256]{2,1,0:T(8,128)(2,1)S(1)}, u32[]{:S(2)}, u32[]{:S(2)}) async-start(bf16[8,32,256]{2,1,0:T(8,128)(2,1)} %all_to_all.26), calls=%async_computation.3 | async-start | bytes 262144 | tf_op jit(solution)/shard_map/all_to_all | solution.py:178
  180.4 0.7 copy-start.9
  181.1 14.8 %all-to-all-start.2 = ((bf16[8,64,256]{2,1,0:T(8,128)(2,1)}), bf16[8,64,256]{2,1,0:T(8,128)(2,1)S(1)}, u32[]{:S(2)}, u32[]{:S(2)}) async-start(bf16[8,64,256]{2,1,0:T(8,128)(2,1)} %copy-done.9), calls=%async_computation.2 | async-start | bytes 524288 | tf_op jit(solution)/shard_map/all_to_all | solution.py:173
Sparse Core Ops, SparseCore 0:
  16.5 27.9 all-gather.4
  46.2 37.6 all-gather.2
